TPU v7x, 256 devices: a whole 4x4x8 slice. The times are simulated.
256 devices in a mesh: hid: 32 (over x, z), tok: 8 (over y, core).
Axes of the slice: x: 4, y: 4, z: 8, core: 2. Of those that a mesh axis runs over, the one named last changes fastest.
Arguments:
- tokens: bfloat16 [2048, 12288], P('tok', 'hid'), may hold values from -6 to 6
- cotangent: bfloat16 [2048, 12288], P('tok', 'hid'), may hold values from -0.75 to 0.75
- up_tiles: bfloat16 [6, 256, 24576], P(None, None, 'hid'), may hold values from -0.15625 to 0.15625
- down_tiles: bfloat16 [6, 24576, 256], P(None, 'hid'), may hold values from -0.109375 to 0.109375
- block_index: int32 [6, 96, 2], P(None, 'hid'), may hold values from 0 to 2, as said below
- up_left: bfloat16 [12288, 256], P('hid'), may hold values from -0.0546875 to 0.0546875
- up_right: bfloat16 [256, 24576], P(None, 'hid'), may hold values from -0.375 to 0.375
- down_left: bfloat16 [24576, 256], P('hid'), may hold values from -0.0390625 to 0.0390625
- down_right: bfloat16 [256, 12288], P(None, 'hid'), may hold values from -0.375 to 0.375
Outputs:
- layer_out: bfloat16 [2048, 12288], P('tok', 'hid')
- grad_tokens: bfloat16 [2048, 12288], P('tok', 'hid')
- grad_up_tiles: bfloat16 [6, 256, 24576], P(None, 'tok', 'hid')
- grad_down_tiles: bfloat16 [6, 24576, 256], P(None, ('hid', 'tok'))
- grad_up_left: bfloat16 [12288, 256], P(('hid', 'tok'))
- grad_up_right: bfloat16 [256, 24576], P('tok', 'hid')
- grad_down_left: bfloat16 [24576, 256], P(('hid', 'tok'))
- grad_down_right: bfloat16 [256, 12288], P('tok', 'hid')
Inputs may be any that keep to these rules, and one draw needn't show every extreme that they name: `block_index`: each row names two different sub-blocks.
All inputs are finite; a program needn't handle non-finite values.
Results may differ from a plain program's by a relative error of at most 0.03.
Values may be sent and summed in bfloat16 or wider, within the bound.
No kernel may reach another device: no remote copies, remote signals or barrier semaphores. Data moves between devices by JAX's collectives and lax.ppermute only.
A program may use at most 128 MiB of HBM per device.

v0:
```python
import jax
import jax.numpy as jnp
from jax import lax
from jax.sharding import PartitionSpec as P

GELU_SCALE = 0.7978845608028654
GELU_CUBIC = 0.044715


def partner(block, axis, distance):
    count = lax.axis_size(axis)
    route = []
    for low in range(count):
        high = low | 1 << distance
        if high != low and high < count:
            route += [(low, high), (high, low)]
    return lax.ppermute(block, axis, route)


def gelu_parts(pre_act):
    inner = GELU_SCALE * (pre_act + GELU_CUBIC * pre_act * pre_act * pre_act)
    tanh_value = jnp.tanh(inner)
    value = 0.5 * pre_act * (1.0 + tanh_value)
    slope = 0.5 * (1.0 + tanh_value) + 0.5 * pre_act * (
        1.0 - tanh_value * tanh_value
    ) * GELU_SCALE * (1.0 + 3.0 * GELU_CUBIC * pre_act * pre_act)
    return (value, slope)


def on_device(
    tokens, cotangent, up_tiles, down_tiles, block_index, up_left, up_right, down_left, down_right
):
    hid_count = lax.axis_size("hid")
    level_count = hid_count.bit_length()
    position = lax.axis_index("hid")
    token_rows, feat_width = tokens.shape
    sub_width = feat_width // 3
    block_count = block_index.shape[1]
    hidden_width = up_tiles.shape[2]
    block_width = hidden_width // block_count
    select_float_values = (block_index[..., None] == jnp.arange(3, dtype=jnp.int32)).astype(
        jnp.float32
    )
    select_half_values = select_float_values.astype(jnp.bfloat16)
    up_blocks = [
        up_tiles[partition_key].reshape(2, sub_width, block_count, block_width)
        for partition_key in range(level_count)
    ]
    down_blocks = [
        down_tiles[partition_key].reshape(block_count, block_width, 2, sub_width)
        for partition_key in range(level_count)
    ]

    def partner_of(partition_key):
        if partition_key == 0:
            return position
        return jnp.bitwise_xor(position, jnp.int32(1 << partition_key - 1))

    def choose(field, partition_key):
        reshaped_tiles = field.reshape(token_rows, 3, sub_width)
        return jnp.einsum(
            "rfg,hyf->rhyg",
            reshaped_tiles,
            select_half_values[partition_key],
            preferred_element_type=jnp.float32,
        ).astype(jnp.bfloat16)

    def place(partner_pairs, partition_key):
        placed_blocks = jnp.einsum(
            "kdow,dog->kgw",
            partner_pairs,
            select_float_values[partition_key],
            precision=lax.Precision.HIGHEST,
        )
        return placed_blocks.reshape(token_rows, feat_width).astype(jnp.bfloat16)

    gathered = lax.all_gather(tokens, "hid", axis=1, tiled=True)
    feature_copies = [
        lax.dynamic_slice_in_dim(gathered, partner_of(partition_key) * feat_width, feat_width, 1)
        for partition_key in range(level_count)
    ]
    low_up = lax.psum(
        jnp.dot(tokens, up_left, preferred_element_type=jnp.float32).astype(jnp.bfloat16), "hid"
    )
    chosen_inputs = [
        choose(feature_copies[partition_key], partition_key) for partition_key in range(level_count)
    ]
    pre_act = jnp.dot(low_up, up_right, preferred_element_type=jnp.float32).reshape(
        token_rows, block_count, block_width
    )
    for partition_key in range(level_count):
        pre_act = pre_act + jnp.einsum(
            "tbjs,jsbh->tbh",
            chosen_inputs[partition_key],
            up_blocks[partition_key],
            preferred_element_type=jnp.float32,
        )
    hidden_value, slope = gelu_parts(pre_act)
    hidden_act = hidden_value.astype(jnp.bfloat16)
    hidden_flat = hidden_act.reshape(token_rows, hidden_width)
    low_down = lax.psum(
        jnp.dot(hidden_flat, down_left, preferred_element_type=jnp.float32).astype(jnp.bfloat16),
        "hid",
    )
    out_parts = [
        place(
            jnp.einsum(
                "tbh,bhjs->tbjs",
                hidden_act,
                down_blocks[partition_key],
                preferred_element_type=jnp.float32,
            ),
            partition_key,
        )
        for partition_key in range(level_count)
    ]
    output_acc = out_parts[0].astype(jnp.float32)
    for partition_key in range(1, level_count):
        output_acc = output_acc + partner(
            out_parts[partition_key], "hid", partition_key - 1
        ).astype(jnp.float32)
    layer_out = (
        output_acc + jnp.dot(low_down, down_right, preferred_element_type=jnp.float32)
    ).astype(jnp.bfloat16)
    back_down = lax.psum(
        jnp.dot(cotangent, down_right.T, preferred_element_type=jnp.float32).astype(jnp.bfloat16),
        "hid",
    )
    grad_gathered = lax.all_gather(cotangent, "hid", axis=1, tiled=True)
    grad_copies = [
        lax.dynamic_slice_in_dim(
            grad_gathered, partner_of(partition_key) * feat_width, feat_width, 1
        )
        for partition_key in range(level_count)
    ]
    chosen_grads = [
        choose(grad_copies[partition_key], partition_key) for partition_key in range(level_count)
    ]
    grad_hidden = jnp.dot(back_down, down_left.T, preferred_element_type=jnp.float32).reshape(
        token_rows, block_count, block_width
    )
    for partition_key in range(level_count):
        grad_hidden = grad_hidden + jnp.einsum(
            "tbjs,bhjs->tbh",
            chosen_grads[partition_key],
            down_blocks[partition_key],
            preferred_element_type=jnp.float32,
        )
    down_terms = jnp.stack(
        [
            jnp.einsum(
                "tbh,tbjs->bhjs",
                hidden_act,
                chosen_grads[partition_key],
                preferred_element_type=jnp.float32,
            ).reshape(hidden_width, 2 * sub_width)
            for partition_key in range(level_count)
        ]
    )
    down_left_term = jnp.dot(hidden_flat.T, back_down, preferred_element_type=jnp.float32)
    down_right_term = jnp.dot(low_down.T, cotangent, preferred_element_type=jnp.float32)
    grad_down_tiles, grad_down_left, grad_down_right = (
        lax.psum_scatter(
            down_terms.astype(jnp.bfloat16), "tok", scatter_dimension=1, tiled=True
        ).astype(jnp.float32),
        lax.psum_scatter(
            down_left_term.astype(jnp.bfloat16), "tok", scatter_dimension=0, tiled=True
        ).astype(jnp.float32),
        lax.psum_scatter(
            down_right_term.astype(jnp.bfloat16), "tok", scatter_dimension=0, tiled=True
        ).astype(jnp.float32),
    )
    grad_pre = (grad_hidden * slope).astype(jnp.bfloat16)
    grad_flat = grad_pre.reshape(token_rows, hidden_width)
    back_up = lax.psum(
        jnp.dot(grad_flat, up_right.T, preferred_element_type=jnp.float32).astype(jnp.bfloat16),
        "hid",
    )
    in_parts = [
        place(
            jnp.einsum(
                "tbh,jsbh->tbjs",
                grad_pre,
                up_blocks[partition_key],
                preferred_element_type=jnp.float32,
            ),
            partition_key,
        )
        for partition_key in range(level_count)
    ]
    input_acc = in_parts[0].astype(jnp.float32)
    for partition_key in range(1, level_count):
        input_acc = input_acc + partner(in_parts[partition_key], "hid", partition_key - 1).astype(
            jnp.float32
        )
    grad_tokens = (
        input_acc + jnp.dot(back_up, up_left.T, preferred_element_type=jnp.float32)
    ).astype(jnp.bfloat16)
    up_terms = jnp.stack(
        [
            jnp.einsum(
                "tbjs,tbh->jsbh",
                chosen_inputs[partition_key],
                grad_pre,
                preferred_element_type=jnp.float32,
            ).reshape(2 * sub_width, hidden_width)
            for partition_key in range(level_count)
        ]
    )
    up_right_term = jnp.dot(low_up.T, grad_flat, preferred_element_type=jnp.float32)
    up_left_term = jnp.dot(tokens.T, back_up, preferred_element_type=jnp.float32)
    grad_up_tiles, grad_up_right, grad_up_left = (
        lax.psum_scatter(
            up_terms.astype(jnp.bfloat16), "tok", scatter_dimension=1, tiled=True
        ).astype(jnp.float32),
        lax.psum_scatter(
            up_right_term.astype(jnp.bfloat16), "tok", scatter_dimension=0, tiled=True
        ).astype(jnp.float32),
        lax.psum_scatter(
            up_left_term.astype(jnp.bfloat16), "tok", scatter_dimension=0, tiled=True
        ).astype(jnp.float32),
    )
    return (
        layer_out,
        grad_tokens,
        grad_up_tiles.astype(jnp.bfloat16),
        grad_down_tiles.astype(jnp.bfloat16),
        grad_up_left.astype(jnp.bfloat16),
        grad_up_right.astype(jnp.bfloat16),
        grad_down_left.astype(jnp.bfloat16),
        grad_down_right.astype(jnp.bfloat16),
    )


def solution(mesh):
    return jax.shard_map(
        on_device,
        mesh=mesh,
        in_specs=(
            P("tok", "hid"),
            P("tok", "hid"),
            P(None, None, "hid"),
            P(None, "hid", None),
            P(None, "hid", None),
            P("hid", None),
            P(None, "hid"),
            P("hid", None),
            P(None, "hid"),
        ),
        out_specs=(
            P("tok", "hid"),
            P("tok", "hid"),
            P(None, "tok", "hid"),
            P(None, ("hid", "tok"), None),
            P(("hid", "tok"), None),
            P("tok", "hid"),
            P(("hid", "tok"), None),
            P("tok", "hid"),
        ),
        check_vma=False,
    )
```

profile of v0, /device:TPU:2, one launch (start us, length us, event | category | flops | bytes accessed | tf_op | source)
XLA Modules:
  0.0 776.2 jit_solution(9446525643140161980)
XLA Ops:
  7.3 2.1 convolution_convert_fusion.29
  16.3 2.2 reshape.191
  18.5 2.1 reshape.190
  20.6 2.3 reshape.189
  25.1 2.5 fusion.172
  30.7 127.4 %all-reduce.7.cloned.1.call-done = (bf16[256,256]{1,0:T(8,128)(2,1)}, bf16[256,256]{1,0:T(8,128)(2,1)}) async-done(((bf16[256,256]{1,0:T(8,128)(2,1)}, bf16[256,256]{1,0:T(8,128)(2,1)}), (bf16[256,256]{1,0:T(8,128)(2,1)}, bf16[256,256]{1,0:T(8,128)(2,1)})) %all-reduce.7.cloned.1.call-update) | async-done | bytes 262160 | tf_op jit(solution)/shard_map/psum | solution.py:82
  158.1 2.1 fusion.175
  160.2 2.2 fusion.176
  162.5 84.4 %all-gather.3.cloned.1.call-done = bf16[256,12288]{0,1:T(8,128)(2,1)} async-done(((bf16[256,384]{0,1:T(8,128)(2,1)}), bf16[256,12288]{0,1:T(8,128)(2,1)}) %all-gather.3.cloned.1.call-update) | async-done | bytes 6291472 | tf_op jit(solution)/shard_map/all_gather | solution.py:77
  246.9 88.8 %all-gather.5.cloned.1.call-done = bf16[256,12288]{0,1:T(8,128)(2,1)} async-done(((bf16[256,384]{0,1:T(8,128)(2,1)}), bf16[256,12288]{0,1:T(8,128)(2,1)}) %all-gather.5.cloned.1.call-update) | async-done | bytes 6291472 | tf_op jit(solution)/shard_map/all_gather | solution.py:129
  335.7 3.0 constant_dynamic-slice_fusion.5
  349.8 2.0 fusion.14
  351.8 2.0 fusion.20
  355.7 2.1 fusion.15
  357.7 2.0 fusion.21
  361.6 2.1 fusion.16
  363.7 2.1 fusion.22
  367.6 2.1 fusion.17
  369.7 2.1 fusion.23
  373.6 2.0 fusion.18
  375.6 2.1 fusion.24
  400.2 2.1 copy.346
  404.6 2.0 convolution_convert_fusion.30
  413.9 4.9 copy.351
  423.4 2.1 fusion.52
  426.2 124.4 %all-reduce.5.cloned.1.call-done = (bf16[256,256]{1,0:T(8,128)(2,1)}, bf16[256,256]{1,0:T(8,128)(2,1)}) async-done(((bf16[256,256]{1,0:T(8,128)(2,1)}, bf16[256,256]{1,0:T(8,128)(2,1)}), (bf16[256,256]{1,0:T(8,128)(2,1)}, bf16[256,256]{1,0:T(8,128)(2,1)})) %all-reduce.5.cloned.1.call-update) | async-done | bytes 262160 | tf_op jit(solution)/shard_map/psum | solution.py:101
  554.2 2.1 convolution_convert_fusion.15
  558.2 2.0 convolution_convert_fusion.13
  560.2 2.2 fusion.36
  562.7 2.1 convolution_convert_fusion.14
  569.3 2.2 copy.359
  571.6 2.0 stack_reshape.57
  573.6 2.2 copy.361
  575.8 2.0 stack_reshape.58
  577.8 2.2 copy.363
  580.0 2.0 stack_reshape.59
  583.0 2.0 copy.314
  591.1 2.1 collective-permute-start.6
  593.2 1.9 convolution_convert_fusion.12
  595.5 2.1 fusion.50
  599.6 2.5 collective-permute-start.7
  633.9 3.1 collective-permute-start.2
  639.6 2.1 add_convert_fusion
  641.7 4.1 collective-permute-done.1
  649.2 10.5 %reduce-scatter.17.cloned.1.call-done = bf16[32,384]{1,0:T(8,128)(2,1)} async-done(((bf16[256,384]{1,0:T(8,128)(2,1)}), bf16[32,384]{1,0:T(8,128)(2,1)}) %reduce-scatter.17.cloned.1.call-update) | async-done | bytes 24592 | tf_op jit(solution)/shard_map/reduce_scatter | solution.py:169
  659.8 35.3 %reduce-scatter.13.cloned.1.call-done = bf16[32,768]{1,0:T(8,128)(2,1)} async-done(((bf16[256,768]{1,0:T(8,128)(2,1)}), bf16[32,768]{1,0:T(8,128)(2,1)}) %reduce-scatter.13.cloned.1.call-update) | async-done | bytes 49168 | tf_op jit(solution)/shard_map/reduce_scatter | solution.py:216
  695.0 35.5 %reduce-scatter.15.cloned.1.call-done = bf16[96,256]{1,0:T(8,128)(2,1)} async-done(((bf16[768,256]{1,0:T(8,128)(2,1)}), bf16[96,256]{1,0:T(8,128)(2,1)}) %reduce-scatter.15.cloned.1.call-update) | async-done | bytes 49168 | tf_op jit(solution)/shard_map/reduce_scatter | solution.py:166
  730.5 38.6 %reduce-scatter.11.cloned.1.call-done = bf16[6,96,256]{2,1,0:T(8,128)(2,1)} async-done(((bf16[6,768,256]{2,1,0:T(8,128)(2,1)}), bf16[6,96,256]{2,1,0:T(8,128)(2,1)}) %reduce-scatter.11.cloned.1.call-update) | async-done | bytes 294928 | tf_op jit(solution)/shard_map/reduce_scatter | solution.py:163
  (289 shorter events, 124.5 us)
Async XLA Ops:
  7.2 150.9 %copy-start = (bf16[256,768]{1,0:T(8,128)(2,1)S(1)}, bf16[256,768]{1,0:T(8,128)(2,1)}, u32[]{:S(2)}) copy-start(bf16[256,768]{1,0:T(8,128)(2,1)} %param.15) | copy-start | bytes 1179652
  7.2 7.8 %copy-start.57 = (s32[6,3,2]{0,2,1:T(2,128)S(1)}, s32[6,3,2]{0,2,1:T(2,128)}, u32[]{:S(2)}) copy-start(s32[6,3,2]{0,2,1:T(2,128)} %param.13) | copy-start | bytes 436
  7.2 7.9 %copy-start.37 = (bf16[6,256,768]{2,1,0:T(8,128)(2,1)S(1)}, bf16[6,256,768]{2,1,0:T(8,128)(2,1)}, u32[]{:S(2)}) copy-start(bf16[6,256,768]{2,1,0:T(8,128)(2,1)} %param.11) | copy-start | bytes 7077892
  7.2 150.9 %all-reduce.7.cloned.1.call-start = ((), (), s32[]{:S(2)}) async-start(), calls=%async_computation.15 | async-start | bytes 524288 | tf_op jit(solution)/shard_map/psum | solution.py:82
  11.3 235.6 %all-gather.3.cloned.1.call-start = ((), (), s32[]{:S(2)}) async-start(), calls=%async_computation.6 | async-start | bytes 6488064 | tf_op jit(solution)/shard_map/all_gather | solution.py:77
  13.1 322.6 %all-gather.5.cloned.1.call-start = ((), (), s32[]{:S(2)}) async-start(), calls=%async_computation.7 | async-start | bytes 6488064 | tf_op jit(solution)/shard_map/all_gather | solution.py:129
  14.9 535.6 %all-reduce.5.cloned.1.call-start = ((), (), s32[]{:S(2)}) async-start(), calls=%async_computation.14 | async-start | bytes 524288 | tf_op jit(solution)/shard_map/psum | solution.py:101
  16.3 6.6 copy-start.41
  23.1 360.5 %copy-start.10 = (bf16[2,128,3,256]{3,2,1,0:T(4,128)(2,1)}, bf16[2,128,3,256]{3,2,1,0:T(4,128)(2,1)S(1)}, u32[]{:S(2)}) copy-start(bf16[2,128,3,256]{3,2,1,0:T(4,128)(2,1)S(1)} %reshape.192) | copy-start | bytes 1179652
  27.9 356.9 %copy-start.2 = (bf16[3,256,2,128]{3,2,1,0:T(2,128)(2,1)}, bf16[3,256,2,128]{3,2,1,0:T(2,128)(2,1)S(1)}, u32[]{:S(2)}) copy-start(bf16[3,256,2,128]{3,2,1,0:T(2,128)(2,1)S(1)} %reshape_squeeze.46) | copy-start | bytes 1179652
  28.0 357.1 %copy-start.4 = (bf16[3,256,2,128]{3,2,1,0:T(2,128)(2,1)}, bf16[3,256,2,128]{3,2,1,0:T(2,128)(2,1)S(1)}, u32[]{:S(2)}) copy-start(bf16[3,256,2,128]{3,2,1,0:T(2,128)(2,1)S(1)} %reshape_squeeze.45) | copy-start | bytes 1179652
  28.1 357.4 %copy-start.6 = (bf16[3,256,2,128]{3,2,1,0:T(2,128)(2,1)}, bf16[3,256,2,128]{3,2,1,0:T(2,128)(2,1)S(1)}, u32[]{:S(2)}) copy-start(bf16[3,256,2,128]{3,2,1,0:T(2,128)(2,1)S(1)} %reshape_squeeze.44) | copy-start | bytes 1179652
  28.2 357.7 %copy-start.8 = (bf16[3,256,2,128]{3,2,1,0:T(2,128)(2,1)}, bf16[3,256,2,128]{3,2,1,0:T(2,128)(2,1)S(1)}, u32[]{:S(2)}) copy-start(bf16[3,256,2,128]{3,2,1,0:T(2,128)(2,1)S(1)} %reshape_squeeze.43) | copy-start | bytes 1179652
  359.8 13.8 %copy-start.56 = (bf16[3,2,3,1]{2,1,0,3:T(2,128)(2,1)S(1)}, bf16[3,2,3,1]{2,1,0,3:T(2,128)(2,1)}, u32[]{:S(2)}) copy-start(bf16[3,2,3,1]{2,1,0,3:T(2,128)(2,1)} %get-tuple-element.77) | copy-start | bytes 112
  365.8 13.7 %copy-start.55 = (bf16[3,2,3,1]{2,1,0,3:T(2,128)(2,1)S(1)}, bf16[3,2,3,1]{2,1,0,3:T(2,128)(2,1)}, u32[]{:S(2)}) copy-start(bf16[3,2,3,1]{2,1,0,3:T(2,128)(2,1)} %get-tuple-element.76) | copy-start | bytes 112
  404.6 5.4 copy-start.48
  409.2 238.3 %reduce-scatter.9.cloned.1.call-start = ((), (), s32[]{:S(2)}) async-start(), calls=%async_computation.8 | async-start | bytes 3538944 | tf_op jit(solution)/shard_map/reduce_scatter | solution.py:213
  418.8 230.4 %reduce-scatter.19.cloned.1.call-start = ((), (), s32[]{:S(2)}) async-start(), calls=%async_computation.13 | async-start | bytes 221184
  423.4 127.2 %copy-start.39 = (bf16[256,384]{1,0:T(8,128)(2,1)S(1)}, bf16[256,384]{1,0:T(8,128)(2,1)}, u32[]{:S(2)}) copy-start(bf16[256,384]{1,0:T(8,128)(2,1)} %param.9) | copy-start | bytes 589828
  425.5 130.8 %copy-start.40 = (bf16[256,384]{1,0:T(8,128)(2,1)S(1)}, bf16[256,384]{1,0:T(8,128)(2,1)}, u32[]{:S(2)}) copy-start(bf16[256,384]{1,0:T(8,128)(2,1)} %param.10) | copy-start | bytes 589828
  554.1 105.6 %reduce-scatter.17.cloned.1.call-start = ((), (), s32[]{:S(2)}) async-start(), calls=%async_computation.12 | async-start | bytes 221184 | tf_op jit(solution)/shard_map/reduce_scatter | solution.py:169
  558.2 6.7 copy-start.47
  558.2 136.9 %reduce-scatter.13.cloned.1.call-start = ((), (), s32[]{:S(2)}) async-start(), calls=%async_computation.10 | async-start | bytes 442368 | tf_op jit(solution)/shard_map/reduce_scatter | solution.py:216
  562.5 5.4 copy-start.46
  562.5 168.0 %reduce-scatter.15.cloned.1.call-start = ((), (), s32[]{:S(2)}) async-start(), calls=%async_computation.11 | async-start | bytes 442368 | tf_op jit(solution)/shard_map/reduce_scatter | solution.py:166
  569.3 12.7 %copy-start.38 = (f32[256,3,128]{2,1,0:T(4,128)S(1)}, f32[256,3,128]{2,1,0:T(4,128)}, u32[]{:S(2)}) copy-start(f32[256,3,128]{2,1,0:T(4,128)} %fusion.36) | copy-start | bytes 1179652
  573.6 11.4 %copy-start.50 = (bf16[256,3,128]{2,1,0:T(4,128)(2,1)S(1)}, bf16[256,3,128]{2,1,0:T(4,128)(2,1)}, u32[]{:S(2)}) copy-start(bf16[256,3,128]{2,1,0:T(4,128)(2,1)} %fusion.52) | copy-start | bytes 589828
  583.0 12.1 %copy-start.14 = (bf16[2,128,3,256]{3,2,1,0:T(4,128)(2,1)S(1)}, bf16[2,128,3,256]{3,2,1,0:T(4,128)(2,1)}, u32[]{:S(2)}) copy-start(bf16[2,128,3,256]{3,2,1,0:T(4,128)(2,1)} %reshape.190) | copy-start | bytes 1179652
  587.6 44.5 %collective-permute-start.5 = (bf16[256,384]{1,0:T(8,128)(2,1)}, bf16[256,384]{1,0:T(8,128)(2,1)}, u32[]{:S(2)}, u32[]{:S(2)}) collective-permute-start(bf16[256,384]{1,0:T(8,128)(2,1)} %copy.313), channel_id=1, source_target_pairs={{0,8},{8,0},{16,24},{24,16},{32,40},{40,32},{48,56},{56,48},{64,72... | collective-permute-start | bytes 589832 | tf_op jit(solution)/shard_map/ppermute | solution.py:17
  591.1 41.5 %collective-permute-start.6 = (bf16[256,384]{1,0:T(8,128)(2,1)}, bf16[256,384]{1,0:T(8,128)(2,1)}, u32[]{:S(2)}, u32[]{:S(2)}) collective-permute-start(bf16[256,384]{1,0:T(8,128)(2,1)} %copy.320), channel_id=1, source_target_pairs={{0,16},{16,0},{8,24},{24,8},{32,48},{48,32},{40,56},{56,40},{64,80... | collective-permute-start | bytes 589832 | tf_op jit(solution)/shard_map/ppermute | solution.py:17
  595.4 7.5 copy-start.42
  595.4 8.3 %copy-start.43 = (bf16[1,768,256]{2,1,0:T(8,128)(2,1)S(1)}, bf16[1,768,256]{2,1,0:T(8,128)(2,1)}, u32[]{:S(2)}) copy-start(bf16[1,768,256]{2,1,0:T(8,128)(2,1)} %stack_reshape.56) | copy-start | bytes 1179652
  595.4 173.7 %reduce-scatter.11.cloned.1.call-start = ((), (), s32[]{:S(2)}) async-start(), calls=%async_computation.9 | async-start | bytes 2654208 | tf_op jit(solution)/shard_map/reduce_scatter | solution.py:163
  599.6 5.7 copy-start.45
  599.6 34.3 %collective-permute-start.7 = (bf16[256,384]{1,0:T(8,128)(2,1)}, bf16[256,384]{1,0:T(8,128)(2,1)}, u32[]{:S(2)}, u32[]{:S(2)}) collective-permute-start(bf16[256,384]{1,0:T(8,128)(2,1)} %copy.326), channel_id=1, source_target_pairs={{0,32},{32,0},{8,40},{40,8},{16,48},{48,16},{24,56},{56,24},{64,96... | collective-permute-start | bytes 589832 | tf_op jit(solution)/shard_map/ppermute | solution.py:17
  610.0 26.9 %collective-permute-start.8 = (bf16[256,384]{1,0:T(8,128)(2,1)S(1)}, bf16[256,384]{1,0:T(8,128)(2,1)S(1)}, u32[]{:S(2)}, u32[]{:S(2)}) collective-permute-start(bf16[256,384]{1,0:T(8,128)(2,1)S(1)} %copy.332), channel_id=1, source_target_pairs={{0,64},{64,0},{8,72},{72,8},{16,80},{80,16},{24,88},{88,24},{32,96... | collective-permute-start | bytes 589832 | tf_op jit(solution)/shard_map/ppermute | solution.py:17
  614.6 24.2 %collective-permute-start.9 = (bf16[256,384]{1,0:T(8,128)(2,1)}, bf16[256,384]{1,0:T(8,128)(2,1)S(1)}, u32[]{:S(2)}, u32[]{:S(2)}) collective-permute-start(bf16[256,384]{1,0:T(8,128)(2,1)} %copy.338), channel_id=1, source_target_pairs={{0,128},{128,0},{8,136},{136,8},{16,144},{144,16},{24,152},{152,24... | collective-permute-start | bytes 589832 | tf_op jit(solution)/shard_map/ppermute | solution.py:17
  628.2 11.4 %copy-start.49 = (f32[256,384]{1,0:T(8,128)S(1)}, f32[256,384]{1,0:T(8,128)}, u32[]{:S(2)}) copy-start(f32[256,384]{1,0:T(8,128)} %copy.314) | copy-start | bytes 1179652
  628.2 11.4 %copy-start.51 = (bf16[384,256]{1,0:T(8,128)(2,1)S(1)}, bf16[384,256]{1,0:T(8,128)(2,1)}, u32[]{:S(2)}) copy-start(bf16[384,256]{1,0:T(8,128)(2,1)} %param.14) | copy-start | bytes 589828
  628.2 11.4 %copy-start.54 = (bf16[256,256]{1,0:T(8,128)(2,1)S(1)}, bf16[256,256]{1,0:T(8,128)(2,1)}, u32[]{:S(2)}) copy-start(bf16[256,256]{1,0:T(8,128)(2,1)} %get-tuple-element.33) | copy-start | bytes 393220
  629.5 17.0 %copy-start.52 = (bf16[256,384]{1,0:T(8,128)(2,1)S(1)}, bf16[256,384]{1,0:T(8,128)(2,1)}, u32[]{:S(2)}) copy-start(bf16[256,384]{1,0:T(8,128)(2,1)} %param.17) | copy-start | bytes 589828
  629.6 17.0 %copy-start.53 = (bf16[256,256]{1,0:T(8,128)(2,1)S(1)}, bf16[256,256]{1,0:T(8,128)(2,1)}, u32[]{:S(2)}) copy-start(bf16[256,256]{1,0:T(8,128)(2,1)} %get-tuple-element.32) | copy-start | bytes 393220
  631.2 137.9 %copy-start.1 = (bf16[256,768]{1,0:T(8,128)(2,1)S(1)}, bf16[256,768]{1,0:T(8,128)(2,1)}, u32[]{:S(2)}) copy-start(bf16[256,768]{1,0:T(8,128)(2,1)} %param.15) | copy-start | bytes 1179652
  632.0 9.7 %collective-permute-start = (bf16[256,384]{1,0:T(8,128)(2,1)}, bf16[256,384]{1,0:T(8,128)(2,1)S(1)}, u32[]{:S(2)}, u32[]{:S(2)}) collective-permute-start(bf16[256,384]{1,0:T(8,128)(2,1)} %copy.251), channel_id=1, source_target_pairs={{0,8},{8,0},{16,24},{24,16},{32,40},{40,32},{48,56},{56,48},{64,72... | collective-permute-start | bytes 589832 | tf_op jit(solution)/shard_map/ppermute | solution.py:17
  632.6 13.2 %collective-permute-start.1 = (bf16[256,384]{1,0:T(8,128)(2,1)}, bf16[256,384]{1,0:T(8,128)(2,1)S(1)}, u32[]{:S(2)}, u32[]{:S(2)}) collective-permute-start(bf16[256,384]{1,0:T(8,128)(2,1)} %copy.258), channel_id=1, source_target_pairs={{0,16},{16,0},{8,24},{24,8},{32,48},{48,32},{40,56},{56,40},{64,80... | collective-permute-start | bytes 589832 | tf_op jit(solution)/shard_map/ppermute | solution.py:17
  633.9 12.6 %collective-permute-start.2 = (bf16[256,384]{1,0:T(8,128)(2,1)}, bf16[256,384]{1,0:T(8,128)(2,1)S(1)}, u32[]{:S(2)}, u32[]{:S(2)}) collective-permute-start(bf16[256,384]{1,0:T(8,128)(2,1)} %copy.264), channel_id=1, source_target_pairs={{0,32},{32,0},{8,40},{40,8},{16,48},{48,16},{24,56},{56,24},{64,96... | collective-permute-start | bytes 589832 | tf_op jit(solution)/shard_map/ppermute | solution.py:17
  637.0 9.6 %collective-permute-start.3 = (bf16[256,384]{1,0:T(8,128)(2,1)}, bf16[256,384]{1,0:T(8,128)(2,1)S(1)}, u32[]{:S(2)}, u32[]{:S(2)}) collective-permute-start(bf16[256,384]{1,0:T(8,128)(2,1)} %copy.270), channel_id=1, source_target_pairs={{0,64},{64,0},{8,72},{72,8},{16,80},{80,16},{24,88},{88,24},{32,96... | collective-permute-start | bytes 589832 | tf_op jit(solution)/shard_map/ppermute | solution.py:17
  638.7 7.8 %collective-permute-start.4 = (bf16[256,384]{1,0:T(8,128)(2,1)}, bf16[256,384]{1,0:T(8,128)(2,1)S(1)}, u32[]{:S(2)}, u32[]{:S(2)}) collective-permute-start(bf16[256,384]{1,0:T(8,128)(2,1)} %copy.276), channel_id=1, source_target_pairs={{0,128},{128,0},{8,136},{136,8},{16,144},{144,16},{24,152},{152,24... | collective-permute-start | bytes 589832 | tf_op jit(solution)/shard_map/ppermute | solution.py:17
  (30 other events, 78.4 us)
Sparse Core Ops, SparseCore 0:
  12.1 145.9 all-reduce.6
  161.3 85.5 all-gather.2
  250.0 85.6 all-gather.4
  409.3 141.2 all-reduce.4
  552.9 36.3 reduce-scatter.8
  592.3 32.1 reduce-scatter.18
  627.7 32.0 reduce-scatter.16
  662.8 32.1 reduce-scatter.12
  698.3 32.1 reduce-scatter.14
  733.5 35.5 reduce-scatter.10
where the time goes:
time: 781 us; the launch traced here: 776 us
  waiting for transfers between devices  550 us (70%)
  local copies, waits for them, and re-layouts  106 us (14%)
  matrix products  87.5 us (11%)
  starting transfers between devices  17 us (2%)
  between operations  15.4 us (2%)
    psum x1, waiting for transfers between devices, on_device(): lax.psum(jnp.dot(tokens, up_left, preferred_element_type=jnp.float32).ast...  127 us
    psum x1, waiting for transfers between devices, on_device(): lax.psum(jnp.dot(hidden_flat, down_left, preferred_element_type=jnp.float...  124 us
    all_gather x1, waiting for transfers between devices, on_device(): grad_gathered = lax.all_gather(cotangent, 'hid', axis=1, tiled=True)  88.8 us
    all_gather x1, waiting for transfers between devices, on_device(): gathered = lax.all_gather(tokens, 'hid', axis=1, tiled=True)  84.4 us
    reduce_scatter x1, waiting for transfers between devices, on_device(): lax.psum_scatter(down_terms.astype(jnp.bfloat16), 'tok', scatter_dimensio...  38.6 us
    reduce_scatter x1, waiting for transfers between devices, on_device(): lax.psum_scatter(down_left_term.astype(jnp.bfloat16), 'tok', scatter_dime...  35.5 us
    reduce_scatter x1, waiting for transfers between devices, on_device(): lax.psum_scatter(up_right_term.astype(jnp.bfloat16), 'tok', scatter_dimen...  35.3 us
    dot_general x12, matrix products, choose(): jnp.einsum('rfg,hyf->rhyg', reshaped_tiles, select_half_values[partition_...  22.3 us
  transfers between devices with their start and end apart: 20, of which 10 were waited for; matrix products, arithmetic and copies ran while one was open for 15% of the time, Pallas kernels for 0%

commit v1 on v0

--- a/solution.py
+++ b/solution.py
@@ -126,7 +126,10 @@
         jnp.dot(cotangent, down_right.T, preferred_element_type=jnp.float32).astype(jnp.bfloat16),
         "hid",
     )
-    grad_gathered = lax.all_gather(cotangent, "hid", axis=1, tiled=True)
+    divide_ladders_on = lambda work_x, link_axis: jnp.concatenate(
+        lax.all_to_all(jnp.stack(lax.axis_size(link_axis) * [work_x]), link_axis, 0, 0), axis=1
+    )
+    grad_gathered = divide_ladders_on(cotangent, link_axis="hid")
     grad_copies = [
         lax.dynamic_slice_in_dim(
             grad_gathered, partner_of(partition_key) * feat_width, feat_width, 1

time: 781 us -> 731 us (0.936)
  waiting for transfers between devices: 550 us -> 487 us
  starting transfers between devices: 17 us -> 28.9 us
    all_gather x1 -> x0, waiting for transfers between devices: 88.8 us -> none  [on_device(): grad_gathered = lax.all_gather(cotangent, 'hid', axis=1, tiled=True)]
    psum x1, waiting for transfers between devices: 127 us -> 153 us  [on_device(): lax.psum(jnp.dot(tokens, up_left, preferred_element_type=jnp.float32).ast...]
    all_to_all x0 -> x1, starting transfers between devices: none -> 11.9 us  [on_device(): lax.all_to_all(jnp.stack(lax.axis_size(link_axis) * [work_x]), link_axis,...]
    unnamed x131 -> x133, local copies, waits for them, and re-layouts: 17.7 us -> 16.1 us
  transfers between devices with their start and end apart: 20 -> 20, of which waited for: 10 -> 9; matrix products, arithmetic and copies ran while one was open for 15% -> 16% of each run, Pallas kernels for 0% -> 0%
where the time goes in v1:
time: 731 us; the launch traced here: 726 us
  waiting for transfers between devices  487 us (67%)
  local copies, waits for them, and re-layouts  108 us (15%)
  matrix products  87.4 us (12%)
  starting transfers between devices  28.9 us (4%)
  between operations  15 us (2%)
    psum x1, waiting for transfers between devices, on_device(): lax.psum(jnp.dot(tokens, up_left, preferred_element_type=jnp.float32).ast...  153 us
    psum x1, waiting for transfers between devices, on_device(): lax.psum(jnp.dot(hidden_flat, down_left, preferred_element_type=jnp.float...  124 us
    all_gather x1, waiting for transfers between devices, on_device(): gathered = lax.all_gather(tokens, 'hid', axis=1, tiled=True)  84.4 us
    reduce_scatter x1, waiting for transfers between devices, on_device(): lax.psum_scatter(down_terms.astype(jnp.bfloat16), 'tok', scatter_dimensio...  38.8 us
    reduce_scatter x1, waiting for transfers between devices, on_device(): lax.psum_scatter(down_left_term.astype(jnp.bfloat16), 'tok', scatter_dime...  35.4 us
    reduce_scatter x1, waiting for transfers between devices, on_device(): lax.psum_scatter(up_right_term.astype(jnp.bfloat16), 'tok', scatter_dimen...  35.3 us
    dot_general x12, matrix products, choose(): jnp.einsum('rfg,hyf->rhyg', reshaped_tiles, select_half_values[partition_...  22.3 us
    reshape x12, local copies, waits for them, and re-layouts, choose(): reshaped_tiles = field.reshape(token_rows, 3, sub_width)  19.9 us
  transfers between devices with their start and end apart: 20, of which 9 were waited for; matrix products, arithmetic and copies ran while one was open for 16% of the time, Pallas kernels for 0%

profile of v1, /device:TPU:2, one launch (start us, length us, event | category | flops | bytes accessed | tf_op | source)
XLA Modules:
  0.0 725.8 jit_solution(15182358376455224441)
XLA Ops:
  7.2 2.0 convolution_convert_fusion.29
  12.2 3.3 stack.8
  15.5 11.9 %all-to-all-start = ((bf16[32,256,384]{1,2,0:T(8,128)(2,1)}), bf16[32,256,384]{1,2,0:T(8,128)(2,1)}, u32[]{:S(2)}, u32[]{:S(2)}) async-start(bf16[32,256,384]{1,2,0:T(8,128)(2,1)} %stack.8), calls=%async_computation | async-start | bytes 12582912 | tf_op jit(solution)/shard_map/all_to_all | solution.py:130
  29.7 2.2 reshape.201
  31.9 2.1 reshape.200
  34.1 2.3 reshape.199
  38.6 2.5 fusion.172
  44.1 152.9 %all-reduce.7.cloned.1.call-done = (bf16[256,256]{1,0:T(8,128)(2,1)}, bf16[256,256]{1,0:T(8,128)(2,1)}) async-done(((bf16[256,256]{1,0:T(8,128)(2,1)}, bf16[256,256]{1,0:T(8,128)(2,1)}), (bf16[256,256]{1,0:T(8,128)(2,1)}, bf16[256,256]{1,0:T(8,128)(2,1)})) %all-reduce.7.cloned.1.call-update) | async-done | bytes 262160 | tf_op jit(solution)/shard_map/psum | solution.py:82
  197.0 2.1 fusion.175
  199.1 2.3 fusion.176
  201.4 84.4 %all-gather.2.cloned.1.call-done = bf16[256,12288]{0,1:T(8,128)(2,1)} async-done(((bf16[256,384]{0,1:T(8,128)(2,1)}), bf16[256,12288]{0,1:T(8,128)(2,1)}) %all-gather.2.cloned.1.call-update) | async-done | bytes 6291472 | tf_op jit(solution)/shard_map/all_gather | solution.py:77
  285.8 3.0 constant_dynamic-slice_fusion.5
  299.8 2.0 fusion.14
  301.8 2.1 fusion.20
  305.7 2.0 fusion.15
  307.7 2.0 fusion.21
  311.5 2.1 fusion.16
  313.6 2.1 fusion.22
  317.5 2.1 fusion.17
  319.6 2.1 fusion.23
  323.5 2.0 fusion.18
  325.5 2.1 fusion.24
  350.1 2.1 copy.346
  354.4 2.0 convolution_convert_fusion.30
  363.8 4.9 copy.351
  373.2 2.1 fusion.52
  376.0 124.4 %all-reduce.5.cloned.1.call-done = (bf16[256,256]{1,0:T(8,128)(2,1)}, bf16[256,256]{1,0:T(8,128)(2,1)}) async-done(((bf16[256,256]{1,0:T(8,128)(2,1)}, bf16[256,256]{1,0:T(8,128)(2,1)}), (bf16[256,256]{1,0:T(8,128)(2,1)}, bf16[256,256]{1,0:T(8,128)(2,1)})) %all-reduce.5.cloned.1.call-update) | async-done | bytes 262160 | tf_op jit(solution)/shard_map/psum | solution.py:101
  504.1 2.1 convolution_convert_fusion.15
  508.1 2.0 convolution_convert_fusion.13
  510.1 2.2 fusion.36
  512.6 2.1 convolution_convert_fusion.14
  519.2 2.2 copy.359
  521.4 2.0 stack_reshape.57
  523.4 2.2 copy.361
  525.7 2.0 stack_reshape.58
  527.7 2.2 copy.363
  529.9 2.0 stack_reshape.59
  532.8 2.0 copy.314
  541.0 2.1 collective-permute-start.6
  545.4 2.1 fusion.50
  549.5 2.5 collective-permute-start.7
  583.8 3.1 collective-permute-start.2
  589.5 2.1 add_convert_fusion
  591.6 4.1 collective-permute-done.1
  599.1 10.4 %reduce-scatter.17.cloned.1.call-done = bf16[32,384]{1,0:T(8,128)(2,1)} async-done(((bf16[256,384]{1,0:T(8,128)(2,1)}), bf16[32,384]{1,0:T(8,128)(2,1)}) %reduce-scatter.17.cloned.1.call-update) | async-done | bytes 24592 | tf_op jit(solution)/shard_map/reduce_scatter | solution.py:172
  609.5 35.3 %reduce-scatter.13.cloned.1.call-done = bf16[32,768]{1,0:T(8,128)(2,1)} async-done(((bf16[256,768]{1,0:T(8,128)(2,1)}), bf16[32,768]{1,0:T(8,128)(2,1)}) %reduce-scatter.13.cloned.1.call-update) | async-done | bytes 49168 | tf_op jit(solution)/shard_map/reduce_scatter | solution.py:219
  644.8 35.4 %reduce-scatter.15.cloned.1.call-done = bf16[96,256]{1,0:T(8,128)(2,1)} async-done(((bf16[768,256]{1,0:T(8,128)(2,1)}), bf16[96,256]{1,0:T(8,128)(2,1)}) %reduce-scatter.15.cloned.1.call-update) | async-done | bytes 49168 | tf_op jit(solution)/shard_map/reduce_scatter | solution.py:169
  680.2 38.8 %reduce-scatter.11.cloned.1.call-done = bf16[6,96,256]{2,1,0:T(8,128)(2,1)} async-done(((bf16[6,768,256]{2,1,0:T(8,128)(2,1)}), bf16[6,96,256]{2,1,0:T(8,128)(2,1)}) %reduce-scatter.11.cloned.1.call-update) | async-done | bytes 294928 | tf_op jit(solution)/shard_map/reduce_scatter | solution.py:166
  (291 shorter events, 124.6 us)
Async XLA Ops:
  7.2 189.8 %copy-start = (bf16[256,768]{1,0:T(8,128)(2,1)S(1)}, bf16[256,768]{1,0:T(8,128)(2,1)}, u32[]{:S(2)}) copy-start(bf16[256,768]{1,0:T(8,128)(2,1)} %param.15) | copy-start | bytes 1179652
  7.2 189.8 %all-reduce.7.cloned.1.call-start = ((), (), s32[]{:S(2)}) async-start(), calls=%async_computation.15 | async-start | bytes 524288 | tf_op jit(solution)/shard_map/psum | solution.py:82
  15.5 12.0 %copy-start.39 = (bf16[256,384]{1,0:T(8,128)(2,1)S(1)}, bf16[256,384]{1,0:T(8,128)(2,1)}, u32[]{:S(2)}) copy-start(bf16[256,384]{1,0:T(8,128)(2,1)} %param.9) | copy-start | bytes 589828
  15.5 12.9 %copy-start.58 = (s32[6,3,2]{0,2,1:T(2,128)S(1)}, s32[6,3,2]{0,2,1:T(2,128)}, u32[]{:S(2)}) copy-start(s32[6,3,2]{0,2,1:T(2,128)} %param.13) | copy-start | bytes 436
  15.5 13.0 %copy-start.37 = (bf16[6,256,768]{2,1,0:T(8,128)(2,1)S(1)}, bf16[6,256,768]{2,1,0:T(8,128)(2,1)}, u32[]{:S(2)}) copy-start(bf16[6,256,768]{2,1,0:T(8,128)(2,1)} %param.11) | copy-start | bytes 7077892
  15.5 185.9 %all-to-all-start = ((bf16[32,256,384]{1,2,0:T(8,128)(2,1)}), bf16[32,256,384]{1,2,0:T(8,128)(2,1)}, u32[]{:S(2)}, u32[]{:S(2)}) async-start(bf16[32,256,384]{1,2,0:T(8,128)(2,1)} %stack.8), calls=%async_computation | async-start | bytes 12582912 | tf_op jit(solution)/shard_map/all_to_all | solution.py:130
  27.4 258.3 %all-gather.2.cloned.1.call-start = ((), (), s32[]{:S(2)}) async-start(), calls=%async_computation.7 | async-start | bytes 6488064 | tf_op jit(solution)/shard_map/all_gather | solution.py:77
  28.3 472.1 %all-reduce.5.cloned.1.call-start = ((), (), s32[]{:S(2)}) async-start(), calls=%async_computation.14 | async-start | bytes 524288 | tf_op jit(solution)/shard_map/psum | solution.py:101
  29.7 6.6 copy-start.42
  36.5 297.0 %copy-start.10 = (bf16[2,128,3,256]{3,2,1,0:T(4,128)(2,1)}, bf16[2,128,3,256]{3,2,1,0:T(4,128)(2,1)S(1)}, u32[]{:S(2)}) copy-start(bf16[2,128,3,256]{3,2,1,0:T(4,128)(2,1)S(1)} %reshape.202) | copy-start | bytes 1179652
  41.3 293.4 %copy-start.2 = (bf16[3,256,2,128]{3,2,1,0:T(2,128)(2,1)}, bf16[3,256,2,128]{3,2,1,0:T(2,128)(2,1)S(1)}, u32[]{:S(2)}) copy-start(bf16[3,256,2,128]{3,2,1,0:T(2,128)(2,1)S(1)} %reshape_squeeze.46) | copy-start | bytes 1179652
  41.4 293.6 %copy-start.4 = (bf16[3,256,2,128]{3,2,1,0:T(2,128)(2,1)}, bf16[3,256,2,128]{3,2,1,0:T(2,128)(2,1)S(1)}, u32[]{:S(2)}) copy-start(bf16[3,256,2,128]{3,2,1,0:T(2,128)(2,1)S(1)} %reshape_squeeze.45) | copy-start | bytes 1179652
  41.5 293.9 %copy-start.6 = (bf16[3,256,2,128]{3,2,1,0:T(2,128)(2,1)}, bf16[3,256,2,128]{3,2,1,0:T(2,128)(2,1)S(1)}, u32[]{:S(2)}) copy-start(bf16[3,256,2,128]{3,2,1,0:T(2,128)(2,1)S(1)} %reshape_squeeze.44) | copy-start | bytes 1179652
  41.6 294.2 %copy-start.8 = (bf16[3,256,2,128]{3,2,1,0:T(2,128)(2,1)}, bf16[3,256,2,128]{3,2,1,0:T(2,128)(2,1)S(1)}, u32[]{:S(2)}) copy-start(bf16[3,256,2,128]{3,2,1,0:T(2,128)(2,1)S(1)} %reshape_squeeze.43) | copy-start | bytes 1179652
  309.7 13.7 %copy-start.57 = (bf16[3,2,3,1]{2,1,0,3:T(2,128)(2,1)S(1)}, bf16[3,2,3,1]{2,1,0,3:T(2,128)(2,1)}, u32[]{:S(2)}) copy-start(bf16[3,2,3,1]{2,1,0,3:T(2,128)(2,1)} %get-tuple-element.77) | copy-start | bytes 112
  315.7 13.7 %copy-start.56 = (bf16[3,2,3,1]{2,1,0,3:T(2,128)(2,1)S(1)}, bf16[3,2,3,1]{2,1,0,3:T(2,128)(2,1)}, u32[]{:S(2)}) copy-start(bf16[3,2,3,1]{2,1,0,3:T(2,128)(2,1)} %get-tuple-element.76) | copy-start | bytes 112
  359.1 238.3 %reduce-scatter.9.cloned.1.call-start = ((), (), s32[]{:S(2)}) async-start(), calls=%async_computation.8 | async-start | bytes 3538944 | tf_op jit(solution)/shard_map/reduce_scatter | solution.py:216
  368.7 230.4 %reduce-scatter.19.cloned.1.call-start = ((), (), s32[]{:S(2)}) async-start(), calls=%async_computation.13 | async-start | bytes 221184
  373.2 127.2 %copy-start.40 = (bf16[256,384]{1,0:T(8,128)(2,1)S(1)}, bf16[256,384]{1,0:T(8,128)(2,1)}, u32[]{:S(2)}) copy-start(bf16[256,384]{1,0:T(8,128)(2,1)} %param.9) | copy-start | bytes 589828
  375.4 130.8 %copy-start.41 = (bf16[256,384]{1,0:T(8,128)(2,1)S(1)}, bf16[256,384]{1,0:T(8,128)(2,1)}, u32[]{:S(2)}) copy-start(bf16[256,384]{1,0:T(8,128)(2,1)} %param.10) | copy-start | bytes 589828
  504.0 105.5 %reduce-scatter.17.cloned.1.call-start = ((), (), s32[]{:S(2)}) async-start(), calls=%async_computation.12 | async-start | bytes 221184 | tf_op jit(solution)/shard_map/reduce_scatter | solution.py:172
  508.0 6.7 copy-start.48
  508.1 136.7 %reduce-scatter.13.cloned.1.call-start = ((), (), s32[]{:S(2)}) async-start(), calls=%async_computation.10 | async-start | bytes 442368 | tf_op jit(solution)/shard_map/reduce_scatter | solution.py:219
  512.4 5.4 copy-start.47
  512.4 167.8 %reduce-scatter.15.cloned.1.call-start = ((), (), s32[]{:S(2)}) async-start(), calls=%async_computation.11 | async-start | bytes 442368 | tf_op jit(solution)/shard_map/reduce_scatter | solution.py:169
  519.2 12.7 %copy-start.38 = (f32[256,3,128]{2,1,0:T(4,128)S(1)}, f32[256,3,128]{2,1,0:T(4,128)}, u32[]{:S(2)}) copy-start(f32[256,3,128]{2,1,0:T(4,128)} %fusion.36) | copy-start | bytes 1179652
  523.4 11.4 %copy-start.51 = (bf16[256,3,128]{2,1,0:T(4,128)(2,1)S(1)}, bf16[256,3,128]{2,1,0:T(4,128)(2,1)}, u32[]{:S(2)}) copy-start(bf16[256,3,128]{2,1,0:T(4,128)(2,1)} %fusion.52) | copy-start | bytes 589828
  532.8 12.1 %copy-start.14 = (bf16[2,128,3,256]{3,2,1,0:T(4,128)(2,1)S(1)}, bf16[2,128,3,256]{3,2,1,0:T(4,128)(2,1)}, u32[]{:S(2)}) copy-start(bf16[2,128,3,256]{3,2,1,0:T(4,128)(2,1)} %reshape.200) | copy-start | bytes 1179652
  537.4 44.5 %collective-permute-start.5 = (bf16[256,384]{1,0:T(8,128)(2,1)}, bf16[256,384]{1,0:T(8,128)(2,1)}, u32[]{:S(2)}, u32[]{:S(2)}) collective-permute-start(bf16[256,384]{1,0:T(8,128)(2,1)} %copy.313), channel_id=1, source_target_pairs={{0,8},{8,0},{16,24},{24,16},{32,40},{40,32},{48,56},{56,48},{64,72... | collective-permute-start | bytes 589832 | tf_op jit(solution)/shard_map/ppermute | solution.py:17
  541.0 41.5 %collective-permute-start.6 = (bf16[256,384]{1,0:T(8,128)(2,1)}, bf16[256,384]{1,0:T(8,128)(2,1)}, u32[]{:S(2)}, u32[]{:S(2)}) collective-permute-start(bf16[256,384]{1,0:T(8,128)(2,1)} %copy.320), channel_id=1, source_target_pairs={{0,16},{16,0},{8,24},{24,8},{32,48},{48,32},{40,56},{56,40},{64,80... | collective-permute-start | bytes 589832 | tf_op jit(solution)/shard_map/ppermute | solution.py:17
  545.3 7.5 %copy-start.43 = (bf16[1,768,256]{2,1,0:T(8,128)(2,1)S(1)}, bf16[1,768,256]{2,1,0:T(8,128)(2,1)}, u32[]{:S(2)}) copy-start(bf16[1,768,256]{2,1,0:T(8,128)(2,1)} %stack_reshape.55) | copy-start | bytes 1179652
  545.3 8.3 %copy-start.44 = (bf16[1,768,256]{2,1,0:T(8,128)(2,1)S(1)}, bf16[1,768,256]{2,1,0:T(8,128)(2,1)}, u32[]{:S(2)}) copy-start(bf16[1,768,256]{2,1,0:T(8,128)(2,1)} %stack_reshape.56) | copy-start | bytes 1179652
  545.4 173.6 %reduce-scatter.11.cloned.1.call-start = ((), (), s32[]{:S(2)}) async-start(), calls=%async_computation.9 | async-start | bytes 2654208 | tf_op jit(solution)/shard_map/reduce_scatter | solution.py:166
  549.5 5.7 copy-start.46
  549.5 34.3 %collective-permute-start.7 = (bf16[256,384]{1,0:T(8,128)(2,1)}, bf16[256,384]{1,0:T(8,128)(2,1)}, u32[]{:S(2)}, u32[]{:S(2)}) collective-permute-start(bf16[256,384]{1,0:T(8,128)(2,1)} %copy.326), channel_id=1, source_target_pairs={{0,32},{32,0},{8,40},{40,8},{16,48},{48,16},{24,56},{56,24},{64,96... | collective-permute-start | bytes 589832 | tf_op jit(solution)/shard_map/ppermute | solution.py:17
  559.9 26.9 %collective-permute-start.8 = (bf16[256,384]{1,0:T(8,128)(2,1)S(1)}, bf16[256,384]{1,0:T(8,128)(2,1)S(1)}, u32[]{:S(2)}, u32[]{:S(2)}) collective-permute-start(bf16[256,384]{1,0:T(8,128)(2,1)S(1)} %copy.332), channel_id=1, source_target_pairs={{0,64},{64,0},{8,72},{72,8},{16,80},{80,16},{24,88},{88,24},{32,96... | collective-permute-start | bytes 589832 | tf_op jit(solution)/shard_map/ppermute | solution.py:17
  564.4 24.2 %collective-permute-start.9 = (bf16[256,384]{1,0:T(8,128)(2,1)}, bf16[256,384]{1,0:T(8,128)(2,1)S(1)}, u32[]{:S(2)}, u32[]{:S(2)}) collective-permute-start(bf16[256,384]{1,0:T(8,128)(2,1)} %copy.338), channel_id=1, source_target_pairs={{0,128},{128,0},{8,136},{136,8},{16,144},{144,16},{24,152},{152,24... | collective-permute-start | bytes 589832 | tf_op jit(solution)/shard_map/ppermute | solution.py:17
  578.1 11.4 %copy-start.50 = (f32[256,384]{1,0:T(8,128)S(1)}, f32[256,384]{1,0:T(8,128)}, u32[]{:S(2)}) copy-start(f32[256,384]{1,0:T(8,128)} %copy.314) | copy-start | bytes 1179652
  578.1 11.4 %copy-start.52 = (bf16[384,256]{1,0:T(8,128)(2,1)S(1)}, bf16[384,256]{1,0:T(8,128)(2,1)}, u32[]{:S(2)}) copy-start(bf16[384,256]{1,0:T(8,128)(2,1)} %param.14) | copy-start | bytes 589828
  578.1 11.4 %copy-start.55 = (bf16[256,256]{1,0:T(8,128)(2,1)S(1)}, bf16[256,256]{1,0:T(8,128)(2,1)}, u32[]{:S(2)}) copy-start(bf16[256,256]{1,0:T(8,128)(2,1)} %get-tuple-element.33) | copy-start | bytes 393220
  579.4 17.0 %copy-start.53 = (bf16[256,384]{1,0:T(8,128)(2,1)S(1)}, bf16[256,384]{1,0:T(8,128)(2,1)}, u32[]{:S(2)}) copy-start(bf16[256,384]{1,0:T(8,128)(2,1)} %param.17) | copy-start | bytes 589828
  579.4 17.0 %copy-start.54 = (bf16[256,256]{1,0:T(8,128)(2,1)S(1)}, bf16[256,256]{1,0:T(8,128)(2,1)}, u32[]{:S(2)}) copy-start(bf16[256,256]{1,0:T(8,128)(2,1)} %get-tuple-element.32) | copy-start | bytes 393220
  581.1 137.9 %copy-start.1 = (bf16[256,768]{1,0:T(8,128)(2,1)S(1)}, bf16[256,768]{1,0:T(8,128)(2,1)}, u32[]{:S(2)}) copy-start(bf16[256,768]{1,0:T(8,128)(2,1)} %param.15) | copy-start | bytes 1179652
  581.9 9.7 %collective-permute-start = (bf16[256,384]{1,0:T(8,128)(2,1)}, bf16[256,384]{1,0:T(8,128)(2,1)S(1)}, u32[]{:S(2)}, u32[]{:S(2)}) collective-permute-start(bf16[256,384]{1,0:T(8,128)(2,1)} %copy.251), channel_id=1, source_target_pairs={{0,8},{8,0},{16,24},{24,16},{32,40},{40,32},{48,56},{56,48},{64,72... | collective-permute-start | bytes 589832 | tf_op jit(solution)/shard_map/ppermute | solution.py:17
  582.5 13.2 %collective-permute-start.1 = (bf16[256,384]{1,0:T(8,128)(2,1)}, bf16[256,384]{1,0:T(8,128)(2,1)S(1)}, u32[]{:S(2)}, u32[]{:S(2)}) collective-permute-start(bf16[256,384]{1,0:T(8,128)(2,1)} %copy.258), channel_id=1, source_target_pairs={{0,16},{16,0},{8,24},{24,8},{32,48},{48,32},{40,56},{56,40},{64,80... | collective-permute-start | bytes 589832 | tf_op jit(solution)/shard_map/ppermute | solution.py:17
  583.8 12.6 %collective-permute-start.2 = (bf16[256,384]{1,0:T(8,128)(2,1)}, bf16[256,384]{1,0:T(8,128)(2,1)S(1)}, u32[]{:S(2)}, u32[]{:S(2)}) collective-permute-start(bf16[256,384]{1,0:T(8,128)(2,1)} %copy.264), channel_id=1, source_target_pairs={{0,32},{32,0},{8,40},{40,8},{16,48},{48,16},{24,56},{56,24},{64,96... | collective-permute-start | bytes 589832 | tf_op jit(solution)/shard_map/ppermute | solution.py:17
  586.8 9.6 %collective-permute-start.3 = (bf16[256,384]{1,0:T(8,128)(2,1)}, bf16[256,384]{1,0:T(8,128)(2,1)S(1)}, u32[]{:S(2)}, u32[]{:S(2)}) collective-permute-start(bf16[256,384]{1,0:T(8,128)(2,1)} %copy.270), channel_id=1, source_target_pairs={{0,64},{64,0},{8,72},{72,8},{16,80},{80,16},{24,88},{88,24},{32,96... | collective-permute-start | bytes 589832 | tf_op jit(solution)/shard_map/ppermute | solution.py:17
  588.6 7.8 %collective-permute-start.4 = (bf16[256,384]{1,0:T(8,128)(2,1)}, bf16[256,384]{1,0:T(8,128)(2,1)S(1)}, u32[]{:S(2)}, u32[]{:S(2)}) collective-permute-start(bf16[256,384]{1,0:T(8,128)(2,1)} %copy.276), channel_id=1, source_target_pairs={{0,128},{128,0},{8,136},{136,8},{16,144},{144,16},{24,152},{152,24... | collective-permute-start | bytes 589832 | tf_op jit(solution)/shard_map/ppermute | solution.py:17
  (31 other events, 83.8 us)
Sparse Core Ops, SparseCore 0:
  12.1 184.8 all-reduce.6
  200.2 85.5 all-gather.1
  359.2 141.2 all-reduce.4
  502.8 36.3 reduce-scatter.8
  542.2 32.1 reduce-scatter.18
  577.4 32.0 reduce-scatter.16
  612.6 32.1 reduce-scatter.12
  648.0 32.1 reduce-scatter.14
  683.4 35.5 reduce-scatter.10
